TPU v7x, 32 devices: a whole 2x2x4 slice. The times are simulated.
32 devices in a mesh: gx: 8 (over z, y), gy: 4 (over x, core).
Axes of the slice: x: 2, y: 2, z: 4, core: 2. Of those that a mesh axis runs over, the one named last changes fastest.
Arguments:
- fluid_vel: float32 [3, 64, 64, 256], P(None, 'gx', 'gy'), may hold values from -6 to 6
- part_pos: float32 [8192, 3, 128], P(('gx', 'gy')), may hold values from 0 to 1
- part_vel: float32 [8192, 3, 128], P(('gx', 'gy')), may hold values from -6 to 6
- brick_owner: int32 [8192, 1], P(('gx', 'gy')), may hold values from 0 to 31; in each aligned block of 256 rows (0 to 255, 256 to 511, ...) at most 16 rows name the same one
- brick_local: int32 [8192], P(('gx', 'gy')), may hold values from 0 to 255
- cell_in_brick: int32 [8192, 128], P(('gx', 'gy')), may hold values from 0 to 127
- pair_self: int32 [2, 16384], P(None, ('gx', 'gy')), may hold values from 0 to 255
- pair_other: int32 [2, 16384], P(None, ('gx', 'gy')), may hold values from 0 to 287
- halo_list: int32 [1024], P(('gx', 'gy')), may hold values from 0 to 255
Outputs:
- fluid_new: float32 [3, 64, 64, 256], P(None, 'gx', 'gy')
- pos_out: float32 [8192, 3, 128], P(('gx', 'gy'))
- vel_out: float32 [8192, 3, 128], P(('gx', 'gy'))
Inputs may be any that keep to these rules, and one draw needn't show every extreme that they name: `brick_owner`: within the 256 blocks of one device (aligned blocks of rows), no tile is named more than 16 times, a bound that some block reaches.
All inputs are finite; a program needn't handle non-finite values.
Results may differ from a plain program's by a relative error of at most 0.0001.
Values sent between devices are 32-bit elements; how exact they have to be, the bound alone decides.
A program may use at most 64 MiB of HBM per device.

v0:
```python
import jax
import jax.numpy as jnp
from jax import lax
from jax.sharding import PartitionSpec as P

SUBSTEPS = 2
BRICK_X = 2
BRICK_Y = 4
BRICK_Z = 16


def padded_2(cells, sides, width, closed):
    for axis, dim in sides:
        count = lax.axis_size(axis)
        ends = count if closed else count - 1
        head = lax.slice_in_dim(cells, 0, width, axis=dim)
        tail = lax.slice_in_dim(cells, cells.shape[dim] - width, cells.shape[dim], axis=dim)
        cells = jnp.concatenate(
            [
                lax.ppermute(tail, axis, [(i, (i + 1) % count) for i in range(ends)]),
                cells,
                lax.ppermute(head, axis, [((i + 1) % count, i) for i in range(ends)]),
            ],
            axis=dim,
        )
    return cells


def pair_force(xa, xb):
    dist2 = 0.0025 + (xa[:, 0, :, None] - xb[:, 0, None, :]) ** 2
    dist2 = dist2 + (xa[:, 1, :, None] - xb[:, 1, None, :]) ** 2
    dist2 = dist2 + (xa[:, 2, :, None] - xb[:, 2, None, :]) ** 2
    dist = jnp.sqrt(dist2)
    coef = 10.0 * jnp.maximum(0.25 - dist, 0.0) / dist
    total = jnp.sum(coef, axis=2)
    pulled = jnp.einsum("gij,gcj->gci", coef, xb, precision=lax.Precision.HIGHEST)
    return xa * total[:, None, :] - pulled


def grid_bricks(grid):
    comps, sizex, sizey, sizez = grid.shape
    parts = grid.reshape(
        comps, sizex // BRICK_X, BRICK_X, sizey // BRICK_Y, BRICK_Y, sizez // BRICK_Z, BRICK_Z
    )
    parts = jnp.transpose(parts, (1, 3, 5, 0, 2, 4, 6))
    return parts.reshape(-1, comps, BRICK_X * BRICK_Y * BRICK_Z)


def brick_grid(bricks, sizex, sizey, sizez):
    comps = bricks.shape[1]
    parts = bricks.reshape(
        sizex // BRICK_X, sizey // BRICK_Y, sizez // BRICK_Z, comps, BRICK_X, BRICK_Y, BRICK_Z
    )
    parts = jnp.transpose(parts, (3, 0, 4, 1, 5, 2, 6))
    return parts.reshape(comps, sizex, sizey, sizez)


def per_device(
    fluid_vel,
    part_pos,
    part_vel,
    brick_owner,
    brick_local,
    cell_in_brick,
    pair_self,
    pair_other,
    halo_list,
):
    rows_x = lax.axis_size("gx")
    rows_y = lax.axis_size("gy")
    tiles = rows_x * rows_y
    blocks = part_pos.shape[0]
    per_brick = BRICK_X * BRICK_Y * BRICK_Z
    capacity = max(3, 2 * blocks // tiles)
    slots = tiles * capacity
    sizex = fluid_vel.shape[1]
    sizey = fluid_vel.shape[2]
    sizez = fluid_vel.shape[3]
    bricks = sizex // BRICK_X * (sizey // BRICK_Y) * (sizez // BRICK_Z)
    loads = jnp.concatenate([jnp.ones((blocks, 1, per_brick), jnp.float32), part_vel], axis=1)
    bunch = min(32, blocks)
    cells_iota = jnp.arange(per_brick, dtype=jnp.int32)
    cell_groups = cell_in_brick.reshape(blocks // bunch, bunch, per_brick)

    def histogram(item):
        load_part, cell_part = item
        onehot = (cell_part[:, :, None] == cells_iota[None, None, :]).astype(jnp.float32)
        return jnp.einsum("qki,qic->qkc", load_part, onehot, precision=lax.Precision.HIGHEST)

    deposit = lax.map(histogram, (loads.reshape(blocks // bunch, bunch, 4, per_brick), cell_groups))
    deposit = deposit.reshape(blocks, 4, per_brick)
    target = brick_owner[:, 0]
    chosen = (target[:, None] == jnp.arange(tiles, dtype=jnp.int32)[None, :]).astype(jnp.float32)
    block_iota = jnp.arange(blocks, dtype=jnp.int32)
    earlier = (block_iota[:, None] > block_iota[None, :]).astype(jnp.float32)
    before = jnp.dot(earlier, chosen, precision=lax.Precision.HIGHEST)
    rank = jnp.sum(before * chosen, axis=1).astype(jnp.int32)
    slot = target * capacity + rank
    placing = (jnp.arange(slots, dtype=jnp.int32)[:, None] == slot[None, :]).astype(jnp.float32)
    send_ids = jnp.dot(
        placing, brick_local.astype(jnp.float32), precision=lax.Precision.HIGHEST
    ).astype(jnp.int32)
    send_dep = jnp.dot(
        placing, deposit.reshape(blocks, 4 * per_brick), precision=lax.Precision.HIGHEST
    ).reshape(slots, 4, per_brick)
    got_ids, got_dep = (
        lax.all_to_all(send_ids, ("gx", "gy"), split_axis=0, concat_axis=0, tiled=True),
        lax.all_to_all(send_dep, ("gx", "gy"), split_axis=0, concat_axis=0, tiled=True),
    )
    gathering = (jnp.arange(bricks, dtype=jnp.int32)[:, None] == got_ids[None, :]).astype(
        jnp.float32
    )
    summed = jnp.dot(
        gathering, got_dep.reshape(slots, 4 * per_brick), precision=lax.Precision.HIGHEST
    )
    dep_grid = brick_grid(summed.reshape(bricks, 4, per_brick), sizex, sizey, sizez)
    count = dep_grid[0]
    momentum = dep_grid[1:]
    solid = 0.5 * count
    voids = 1.0 - 0.6 * solid / (1.0 + solid)
    beta = (1.0 - voids) / (voids * voids)
    padded = padded_2(fluid_vel, (("gx", 1), ("gy", 2)), 1, False)
    padded = jnp.pad(padded, ((0, 0), (0, 0), (0, 0), (1, 1)))
    beside = padded[:, 2:, 1:-1, 1:-1] + padded[:, :-2, 1:-1, 1:-1]
    beside = beside + padded[:, 1:-1, 2:, 1:-1] + padded[:, 1:-1, :-2, 1:-1]
    beside = beside + padded[:, 1:-1, 1:-1, 2:] + padded[:, 1:-1, 1:-1, :-2]
    lap = beside - 6.0 * fluid_vel
    fluid_new = fluid_vel + 0.1 * lap + 0.15 * beta[None] * (momentum - count[None] * fluid_vel)
    table = grid_bricks(jnp.concatenate([fluid_new, beta[None]], axis=0))
    answer = table[got_ids]
    back = lax.all_to_all(answer, ("gx", "gy"), split_axis=0, concat_axis=0, tiled=True)
    mine = back[slot]

    def pick_cells(item):
        fluid_part, cell_part = item
        onehot = (cell_part[:, :, None] == cells_iota[None, None, :]).astype(jnp.float32)
        return jnp.einsum("qkc,qic->qki", fluid_part, onehot, precision=lax.Precision.HIGHEST)

    local_fluid = lax.map(
        pick_cells, (mine.reshape(blocks // bunch, bunch, 4, per_brick), cell_groups)
    )
    local_fluid = local_fluid.reshape(blocks, 4, per_brick)
    flow = local_fluid[:, :3, :]
    drift = 2.0 * local_fluid[:, 3:4, :]
    down = jnp.array([0.0, 0.0, -1.0], jnp.float32)[None, :, None]
    width = halo_list.shape[0] // 2
    pair_count = pair_self.shape[1]
    group = min(64, pair_count)
    position = part_pos
    velocity = part_vel
    for step in range(SUBSTEPS):
        outgoing = position[halo_list]
        rims = padded_2(outgoing, (("gx", 0),), width, True)
        extended = jnp.concatenate([position, rims[:width], rims[3 * width :]], axis=0)
        firsts = pair_self[step]
        seconds = pair_other[step]

        def one_group(pair):
            return pair_force(extended[pair[0]], extended[pair[1]])

        forces = lax.map(one_group, (firsts.reshape(-1, group), seconds.reshape(-1, group)))
        forces = forces.reshape(pair_count, 3 * per_brick)
        members = (firsts[None, :] == block_iota[:, None]).astype(jnp.float32)
        push = jnp.dot(members, forces, precision=lax.Precision.HIGHEST).reshape(
            blocks, 3, per_brick
        )
        velocity = velocity + 0.1 * (push + drift * (flow - velocity) + down)
        position = position + 0.1 * velocity
    return (fluid_new, position, velocity)


def solution(mesh):
    in_specs = (
        P(None, "gx", "gy", None),
        P(("gx", "gy"), None, None),
        P(("gx", "gy"), None, None),
        P(("gx", "gy"), None),
        P(("gx", "gy")),
        P(("gx", "gy"), None),
        P(None, ("gx", "gy")),
        P(None, ("gx", "gy")),
        P(("gx", "gy")),
    )
    out_specs = (
        P(None, "gx", "gy", None),
        P(("gx", "gy"), None, None),
        P(("gx", "gy"), None, None),
    )
    return jax.shard_map(
        per_device, mesh=mesh, in_specs=in_specs, out_specs=out_specs, check_vma=False
    )
```

profile of v0, /device:TPU:0, one launch (start us, length us, event | category | flops | bytes accessed | tf_op | source)
XLA Modules:
  0.0 454.5 jit_solution(7153842913900019702)
XLA Ops:
  1.5 4.9 %collective-permute-start.1 = (f32[3,1,16,256]{3,2,1,0:T(8,128)S(1)}, f32[3,1,16,256]{3,2,1,0:T(8,128)S(1)}, u32[]{:S(2)}, u32[]{:S(2)}) collective-permute-start(f32[3,1,16,256]{3,2,1,0:T(8,128)S(1)} %get-tuple-element.220), channel_id=1, source_target_pairs={{0,4},{4,8},{8,12},{12,16},{16,20},{20,24},{24,28},{1,5},{5,9},{9,... | collective-permute-start | bytes 147464 | tf_op jit(solution)/shard_map/ppermute | solution.py:20
  11.0 7.0 %all-to-all-start = ((s32[32,16,1]{1,2,0:T(1,128)}), s32[32,16,1]{1,2,0:T(1,128)S(1)}, u32[]{:S(2)}, u32[]{:S(2)}) async-start(s32[32,16,1]{1,2,0:T(1,128)} %bitcast.25), calls=%async_computation | async-start | bytes 32768 | tf_op jit(solution)/shard_map/all_to_all | solution.py:107
  19.4 17.7 %while.44 = (s32[]{:T(128)}, f32[8,32,4,128]{3,2,1,0:T(4,128)S(1)}, f32[8,32,4,128]{3,2,1,0:T(4,128)S(1)}, s32[8,32,128]{2,1,0:T(8,128)}, s32[]{:T(128)}) while((s32[]{:T(128)}, f32[8,32,4,128]{3,2,1,0:T(4,128)S(1)}, f32[8,32,4,128]{3,2,1,0:T(4,128)S(1)}, s32[8,32,128]{2,1,0:T(8,128)}, s32[]{:T(128)}) %tuple.124), condition=%wide.region_2.3_spmd.clone, body=%wide.region_1.2_spmd.clone.sunk | while | flops 25690112 | bytes 181313 | solution.py:90
  39.8 5.8 %all-to-all-start.1 = ((f32[512,4,128]{2,1,0:T(4,128)}), f32[512,4,128]{2,1,0:T(4,128)S(1)}, u32[]{:S(2)}, u32[]{:S(2)}) async-start(f32[512,4,128]{2,1,0:T(4,128)} %copy.60), calls=%async_computation.1 | async-start | bytes 2097152 | tf_op jit(solution)/shard_map/all_to_all | solution.py:108
  49.5 3.0 collective-permute-start.5
  54.7 14.0 %collective-permute-done.4 = f32[16,3,128]{2,0,1:T(8,128)S(1)} collective-permute-done((f32[16,3,128]{2,0,1:T(8,128)S(1)}, f32[16,3,128]{2,0,1:T(8,128)S(1)}, u32[]{:S(2)}, u32[]{:S(2)}) %collective-permute-start.4) | collective-permute-done | bytes 24608 | tf_op jit(solution)/shard_map/ppermute | solution.py:20
  70.3 3.0 collective-permute-start.3
  76.4 3.5 convolution_bitcast_fusion
  83.3 2.5 squeeze.36
  87.4 1.9 copy.63
  89.3 2.8 slice.128
  92.1 3.3 fusion.64
  95.4 1.9 concatenate.41
  99.2 3.0 maximum_bitcast_fusion
  102.2 4.2 reshape.265
  106.8 2.6 gather_fusion.5
  109.4 8.7 %all-to-all-start.2 = ((f32[512,4,128]{2,1,0:T(4,128)}), f32[512,4,128]{2,1,0:T(4,128)}, u32[]{:S(2)}, u32[]{:S(2)}) async-start(f32[512,4,128]{2,1,0:T(4,128)} %gather_fusion.5), calls=%async_computation.2 | async-start | bytes 2097152 | tf_op jit(solution)/shard_map/all_to_all | solution.py:131
  118.3 154.5 %while.42 = (s32[]{:T(128)}, f32[8,64,3,128]{3,2,1,0:T(4,128)S(1)}, s32[8,64]{1,0:T(8,128)S(1)}, f32[288,3,128]{2,1,0:T(4,128)}, s32[8,64]{1,0:T(8,128)S(1)}, /*index=5*/s32[]{:T(128)}) while((s32[]{:T(128)}, f32[8,64,3,128]{3,2,1,0:T(4,128)S(1)}, s32[8,64]{1,0:T(8,128)S(1)}, f32[288,3,128]{2,1,0:T(4,128)}, s32[8,64]{1,0:T(8,128)S(1)}, ...), condition=%wide.region_5.6_spmd, body=%wide.region_3.5_spmd.sunk | while | flops 66103680 | bytes 1648717 | solution.py:161
  121.9 5.3 %fusion.111 = f32[64,128]{1,0:T(8,128)S(1)} fusion(f32[64,128]{1,0:T(8,128)S(1)} %bitcast.224, f32[64,128]{1,0:T(8,128)S(1)} %bitcast.236, f32[64,128]{1,0:T(8,128)S(1)} %bitcast.226, f32[64,128]{1,0:T(8,128)S(1)} %bitcast.238, f32[64,128]{1,0:T(8,128)S(1)} %bitcast.222, f32[64,128]{1,0:T(8,128)S(1)} %bitcast.234), kind=kLoop, calls=%fused_computation.12.clone.1 | loop fusion | flops 14671872 | bytes 229376 | tf_op jit(solution)/shard_map/while/body/eval_jaxpr/reduce_sum | solution.py:35
  127.2 10.3 %fusion.112 = f32[8,64,3,128]{3,2,1,0:T(4,128)S(1)} fusion(f32[8,64,3,128]{3,2,1,0:T(4,128)S(1)} %get-tuple-element.418, s32[]{:T(128)} %get-tuple-element.417, f32[64,3,128]{2,1,0:T(4,128)S(1)} %gather_fusion, f32[64,128]{1,0:T(8,128)S(1)} %bitcast.225, f32[64,128]{1,0:T(8,128)S(1)} %bitcast.237, f32[64,128]{1,0:T(8,128)S(1)} %bitcast.227, ...), kind=kOutput, calls=%fused_computation.15.clone.1 | convolution fusion | flops 51429376 | bytes 622596 | tf_op jit(solution)/shard_map/while/body/eval_jaxpr/gij,gcj->gci/dot_general | solution.py:36
  141.2 5.3 %fusion.111 = f32[64,128]{1,0:T(8,128)S(1)} fusion(f32[64,128]{1,0:T(8,128)S(1)} %bitcast.224, f32[64,128]{1,0:T(8,128)S(1)} %bitcast.236, f32[64,128]{1,0:T(8,128)S(1)} %bitcast.226, f32[64,128]{1,0:T(8,128)S(1)} %bitcast.238, f32[64,128]{1,0:T(8,128)S(1)} %bitcast.222, f32[64,128]{1,0:T(8,128)S(1)} %bitcast.234), kind=kLoop, calls=%fused_computation.12.clone.1 | loop fusion | flops 14671872 | bytes 229376 | tf_op jit(solution)/shard_map/while/body/eval_jaxpr/reduce_sum | solution.py:35
  146.5 10.3 %fusion.112 = f32[8,64,3,128]{3,2,1,0:T(4,128)S(1)} fusion(f32[8,64,3,128]{3,2,1,0:T(4,128)S(1)} %get-tuple-element.418, s32[]{:T(128)} %get-tuple-element.417, f32[64,3,128]{2,1,0:T(4,128)S(1)} %gather_fusion, f32[64,128]{1,0:T(8,128)S(1)} %bitcast.225, f32[64,128]{1,0:T(8,128)S(1)} %bitcast.237, f32[64,128]{1,0:T(8,128)S(1)} %bitcast.227, ...), kind=kOutput, calls=%fused_computation.15.clone.1 | convolution fusion | flops 51429376 | bytes 622596 | tf_op jit(solution)/shard_map/while/body/eval_jaxpr/gij,gcj->gci/dot_general | solution.py:36
  160.6 5.3 %fusion.111 = f32[64,128]{1,0:T(8,128)S(1)} fusion(f32[64,128]{1,0:T(8,128)S(1)} %bitcast.224, f32[64,128]{1,0:T(8,128)S(1)} %bitcast.236, f32[64,128]{1,0:T(8,128)S(1)} %bitcast.226, f32[64,128]{1,0:T(8,128)S(1)} %bitcast.238, f32[64,128]{1,0:T(8,128)S(1)} %bitcast.222, f32[64,128]{1,0:T(8,128)S(1)} %bitcast.234), kind=kLoop, calls=%fused_computation.12.clone.1 | loop fusion | flops 14671872 | bytes 229376 | tf_op jit(solution)/shard_map/while/body/eval_jaxpr/reduce_sum | solution.py:35
  165.9 10.3 %fusion.112 = f32[8,64,3,128]{3,2,1,0:T(4,128)S(1)} fusion(f32[8,64,3,128]{3,2,1,0:T(4,128)S(1)} %get-tuple-element.418, s32[]{:T(128)} %get-tuple-element.417, f32[64,3,128]{2,1,0:T(4,128)S(1)} %gather_fusion, f32[64,128]{1,0:T(8,128)S(1)} %bitcast.225, f32[64,128]{1,0:T(8,128)S(1)} %bitcast.237, f32[64,128]{1,0:T(8,128)S(1)} %bitcast.227, ...), kind=kOutput, calls=%fused_computation.15.clone.1 | convolution fusion | flops 51429376 | bytes 622596 | tf_op jit(solution)/shard_map/while/body/eval_jaxpr/gij,gcj->gci/dot_general | solution.py:36
  179.9 5.3 %fusion.111 = f32[64,128]{1,0:T(8,128)S(1)} fusion(f32[64,128]{1,0:T(8,128)S(1)} %bitcast.224, f32[64,128]{1,0:T(8,128)S(1)} %bitcast.236, f32[64,128]{1,0:T(8,128)S(1)} %bitcast.226, f32[64,128]{1,0:T(8,128)S(1)} %bitcast.238, f32[64,128]{1,0:T(8,128)S(1)} %bitcast.222, f32[64,128]{1,0:T(8,128)S(1)} %bitcast.234), kind=kLoop, calls=%fused_computation.12.clone.1 | loop fusion | flops 14671872 | bytes 229376 | tf_op jit(solution)/shard_map/while/body/eval_jaxpr/reduce_sum | solution.py:35
  185.2 10.3 %fusion.112 = f32[8,64,3,128]{3,2,1,0:T(4,128)S(1)} fusion(f32[8,64,3,128]{3,2,1,0:T(4,128)S(1)} %get-tuple-element.418, s32[]{:T(128)} %get-tuple-element.417, f32[64,3,128]{2,1,0:T(4,128)S(1)} %gather_fusion, f32[64,128]{1,0:T(8,128)S(1)} %bitcast.225, f32[64,128]{1,0:T(8,128)S(1)} %bitcast.237, f32[64,128]{1,0:T(8,128)S(1)} %bitcast.227, ...), kind=kOutput, calls=%fused_computation.15.clone.1 | convolution fusion | flops 51429376 | bytes 622596 | tf_op jit(solution)/shard_map/while/body/eval_jaxpr/gij,gcj->gci/dot_general | solution.py:36
  199.2 5.3 %fusion.111 = f32[64,128]{1,0:T(8,128)S(1)} fusion(f32[64,128]{1,0:T(8,128)S(1)} %bitcast.224, f32[64,128]{1,0:T(8,128)S(1)} %bitcast.236, f32[64,128]{1,0:T(8,128)S(1)} %bitcast.226, f32[64,128]{1,0:T(8,128)S(1)} %bitcast.238, f32[64,128]{1,0:T(8,128)S(1)} %bitcast.222, f32[64,128]{1,0:T(8,128)S(1)} %bitcast.234), kind=kLoop, calls=%fused_computation.12.clone.1 | loop fusion | flops 14671872 | bytes 229376 | tf_op jit(solution)/shard_map/while/body/eval_jaxpr/reduce_sum | solution.py:35
  204.5 10.3 %fusion.112 = f32[8,64,3,128]{3,2,1,0:T(4,128)S(1)} fusion(f32[8,64,3,128]{3,2,1,0:T(4,128)S(1)} %get-tuple-element.418, s32[]{:T(128)} %get-tuple-element.417, f32[64,3,128]{2,1,0:T(4,128)S(1)} %gather_fusion, f32[64,128]{1,0:T(8,128)S(1)} %bitcast.225, f32[64,128]{1,0:T(8,128)S(1)} %bitcast.237, f32[64,128]{1,0:T(8,128)S(1)} %bitcast.227, ...), kind=kOutput, calls=%fused_computation.15.clone.1 | convolution fusion | flops 51429376 | bytes 622596 | tf_op jit(solution)/shard_map/while/body/eval_jaxpr/gij,gcj->gci/dot_general | solution.py:36
  218.5 5.3 %fusion.111 = f32[64,128]{1,0:T(8,128)S(1)} fusion(f32[64,128]{1,0:T(8,128)S(1)} %bitcast.224, f32[64,128]{1,0:T(8,128)S(1)} %bitcast.236, f32[64,128]{1,0:T(8,128)S(1)} %bitcast.226, f32[64,128]{1,0:T(8,128)S(1)} %bitcast.238, f32[64,128]{1,0:T(8,128)S(1)} %bitcast.222, f32[64,128]{1,0:T(8,128)S(1)} %bitcast.234), kind=kLoop, calls=%fused_computation.12.clone.1 | loop fusion | flops 14671872 | bytes 229376 | tf_op jit(solution)/shard_map/while/body/eval_jaxpr/reduce_sum | solution.py:35
  223.8 10.3 %fusion.112 = f32[8,64,3,128]{3,2,1,0:T(4,128)S(1)} fusion(f32[8,64,3,128]{3,2,1,0:T(4,128)S(1)} %get-tuple-element.418, s32[]{:T(128)} %get-tuple-element.417, f32[64,3,128]{2,1,0:T(4,128)S(1)} %gather_fusion, f32[64,128]{1,0:T(8,128)S(1)} %bitcast.225, f32[64,128]{1,0:T(8,128)S(1)} %bitcast.237, f32[64,128]{1,0:T(8,128)S(1)} %bitcast.227, ...), kind=kOutput, calls=%fused_computation.15.clone.1 | convolution fusion | flops 51429376 | bytes 622596 | tf_op jit(solution)/shard_map/while/body/eval_jaxpr/gij,gcj->gci/dot_general | solution.py:36
  237.8 5.3 %fusion.111 = f32[64,128]{1,0:T(8,128)S(1)} fusion(f32[64,128]{1,0:T(8,128)S(1)} %bitcast.224, f32[64,128]{1,0:T(8,128)S(1)} %bitcast.236, f32[64,128]{1,0:T(8,128)S(1)} %bitcast.226, f32[64,128]{1,0:T(8,128)S(1)} %bitcast.238, f32[64,128]{1,0:T(8,128)S(1)} %bitcast.222, f32[64,128]{1,0:T(8,128)S(1)} %bitcast.234), kind=kLoop, calls=%fused_computation.12.clone.1 | loop fusion | flops 14671872 | bytes 229376 | tf_op jit(solution)/shard_map/while/body/eval_jaxpr/reduce_sum | solution.py:35
  243.1 10.3 %fusion.112 = f32[8,64,3,128]{3,2,1,0:T(4,128)S(1)} fusion(f32[8,64,3,128]{3,2,1,0:T(4,128)S(1)} %get-tuple-element.418, s32[]{:T(128)} %get-tuple-element.417, f32[64,3,128]{2,1,0:T(4,128)S(1)} %gather_fusion, f32[64,128]{1,0:T(8,128)S(1)} %bitcast.225, f32[64,128]{1,0:T(8,128)S(1)} %bitcast.237, f32[64,128]{1,0:T(8,128)S(1)} %bitcast.227, ...), kind=kOutput, calls=%fused_computation.15.clone.1 | convolution fusion | flops 51429376 | bytes 622596 | tf_op jit(solution)/shard_map/while/body/eval_jaxpr/gij,gcj->gci/dot_general | solution.py:36
  257.1 5.3 %fusion.111 = f32[64,128]{1,0:T(8,128)S(1)} fusion(f32[64,128]{1,0:T(8,128)S(1)} %bitcast.224, f32[64,128]{1,0:T(8,128)S(1)} %bitcast.236, f32[64,128]{1,0:T(8,128)S(1)} %bitcast.226, f32[64,128]{1,0:T(8,128)S(1)} %bitcast.238, f32[64,128]{1,0:T(8,128)S(1)} %bitcast.222, f32[64,128]{1,0:T(8,128)S(1)} %bitcast.234), kind=kLoop, calls=%fused_computation.12.clone.1 | loop fusion | flops 14671872 | bytes 229376 | tf_op jit(solution)/shard_map/while/body/eval_jaxpr/reduce_sum | solution.py:35
  262.4 10.3 %fusion.112 = f32[8,64,3,128]{3,2,1,0:T(4,128)S(1)} fusion(f32[8,64,3,128]{3,2,1,0:T(4,128)S(1)} %get-tuple-element.418, s32[]{:T(128)} %get-tuple-element.417, f32[64,3,128]{2,1,0:T(4,128)S(1)} %gather_fusion, f32[64,128]{1,0:T(8,128)S(1)} %bitcast.225, f32[64,128]{1,0:T(8,128)S(1)} %bitcast.237, f32[64,128]{1,0:T(8,128)S(1)} %bitcast.227, ...), kind=kOutput, calls=%fused_computation.15.clone.1 | convolution fusion | flops 51429376 | bytes 622596 | tf_op jit(solution)/shard_map/while/body/eval_jaxpr/gij,gcj->gci/dot_general | solution.py:36
  273.2 2.4 gather_fusion.6
  275.6 26.9 %while.45 = (s32[]{:T(128)}, f32[8,32,4,128]{3,1,0,2:T(8,128)}, f32[8,32,4,128]{3,2,1,0:T(4,128)S(1)}, s32[8,32,128]{2,1,0:T(8,128)}, s32[]{:T(128)}) while((s32[]{:T(128)}, f32[8,32,4,128]{3,1,0,2:T(8,128)}, f32[8,32,4,128]{3,2,1,0:T(4,128)S(1)}, s32[8,32,128]{2,1,0:T(8,128)}, s32[]{:T(128)}) %tuple.125), condition=%wide.region_7.8_spmd.clone, body=%wide.region_6.7_spmd.clone.sunk | while | flops 25690112 | bytes 311877 | solution.py:139
  276.3 2.0 fusion.122
  279.7 2.0 fusion.122
  283.0 2.0 fusion.122
  286.4 2.0 fusion.122
  289.7 2.0 fusion.122
  293.1 2.0 fusion.122
  296.4 2.0 fusion.122
  299.8 2.0 fusion.122
  303.4 2.5 multiply_add_fusion.1
  308.5 3.2 collective-permute-start.7
  314.0 137.5 %while.43 = (s32[]{:T(128)}, f32[8,64,3,128]{3,2,1,0:T(4,128)S(1)}, s32[8,64]{1,0:T(8,128)S(1)}, f32[288,3,128]{2,1,0:T(4,128)S(1)}, s32[8,64]{1,0:T(8,128)S(1)}, /*index=5*/s32[]{:T(128)}) while((s32[]{:T(128)}, f32[8,64,3,128]{3,2,1,0:T(4,128)S(1)}, s32[8,64]{1,0:T(8,128)S(1)}, f32[288,3,128]{2,1,0:T(4,128)S(1)}, s32[8,64]{1,0:T(8,128)S(1)}, ...), condition=%wide.region_10.11_spmd, body=%wide.region_8.10_spmd.sunk | while | flops 66103680 | bytes 1648717 | solution.py:161
  315.5 5.3 %fusion.117 = f32[64,128]{1,0:T(8,128)S(1)} fusion(f32[64,128]{1,0:T(8,128)S(1)} %bitcast.230, f32[64,128]{1,0:T(8,128)S(1)} %bitcast.242, f32[64,128]{1,0:T(8,128)S(1)} %bitcast.232, f32[64,128]{1,0:T(8,128)S(1)} %bitcast.244, f32[64,128]{1,0:T(8,128)S(1)} %bitcast.228, f32[64,128]{1,0:T(8,128)S(1)} %bitcast.240), kind=kLoop, calls=%fused_computation.32.clone.1 | loop fusion | flops 14671872 | bytes 229376 | tf_op jit(solution)/shard_map/while/body/eval_jaxpr/reduce_sum | solution.py:35
  320.9 10.3 %fusion.118 = f32[8,64,3,128]{3,2,1,0:T(4,128)S(1)} fusion(f32[8,64,3,128]{3,2,1,0:T(4,128)S(1)} %get-tuple-element.436, s32[]{:T(128)} %get-tuple-element.435, f32[64,3,128]{2,1,0:T(4,128)S(1)} %gather_fusion.2, f32[64,128]{1,0:T(8,128)S(1)} %bitcast.231, f32[64,128]{1,0:T(8,128)S(1)} %bitcast.243, f32[64,128]{1,0:T(8,128)S(1)} %bitcast.233, ...), kind=kOutput, calls=%fused_computation.35.clone.1 | convolution fusion | flops 51429376 | bytes 622596 | tf_op jit(solution)/shard_map/while/body/eval_jaxpr/gij,gcj->gci/dot_general | solution.py:36
  332.7 5.3 %fusion.117 = f32[64,128]{1,0:T(8,128)S(1)} fusion(f32[64,128]{1,0:T(8,128)S(1)} %bitcast.230, f32[64,128]{1,0:T(8,128)S(1)} %bitcast.242, f32[64,128]{1,0:T(8,128)S(1)} %bitcast.232, f32[64,128]{1,0:T(8,128)S(1)} %bitcast.244, f32[64,128]{1,0:T(8,128)S(1)} %bitcast.228, f32[64,128]{1,0:T(8,128)S(1)} %bitcast.240), kind=kLoop, calls=%fused_computation.32.clone.1 | loop fusion | flops 14671872 | bytes 229376 | tf_op jit(solution)/shard_map/while/body/eval_jaxpr/reduce_sum | solution.py:35
  338.0 10.3 %fusion.118 = f32[8,64,3,128]{3,2,1,0:T(4,128)S(1)} fusion(f32[8,64,3,128]{3,2,1,0:T(4,128)S(1)} %get-tuple-element.436, s32[]{:T(128)} %get-tuple-element.435, f32[64,3,128]{2,1,0:T(4,128)S(1)} %gather_fusion.2, f32[64,128]{1,0:T(8,128)S(1)} %bitcast.231, f32[64,128]{1,0:T(8,128)S(1)} %bitcast.243, f32[64,128]{1,0:T(8,128)S(1)} %bitcast.233, ...), kind=kOutput, calls=%fused_computation.35.clone.1 | convolution fusion | flops 51429376 | bytes 622596 | tf_op jit(solution)/shard_map/while/body/eval_jaxpr/gij,gcj->gci/dot_general | solution.py:36
  349.9 5.3 %fusion.117 = f32[64,128]{1,0:T(8,128)S(1)} fusion(f32[64,128]{1,0:T(8,128)S(1)} %bitcast.230, f32[64,128]{1,0:T(8,128)S(1)} %bitcast.242, f32[64,128]{1,0:T(8,128)S(1)} %bitcast.232, f32[64,128]{1,0:T(8,128)S(1)} %bitcast.244, f32[64,128]{1,0:T(8,128)S(1)} %bitcast.228, f32[64,128]{1,0:T(8,128)S(1)} %bitcast.240), kind=kLoop, calls=%fused_computation.32.clone.1 | loop fusion | flops 14671872 | bytes 229376 | tf_op jit(solution)/shard_map/while/body/eval_jaxpr/reduce_sum | solution.py:35
  355.2 10.3 %fusion.118 = f32[8,64,3,128]{3,2,1,0:T(4,128)S(1)} fusion(f32[8,64,3,128]{3,2,1,0:T(4,128)S(1)} %get-tuple-element.436, s32[]{:T(128)} %get-tuple-element.435, f32[64,3,128]{2,1,0:T(4,128)S(1)} %gather_fusion.2, f32[64,128]{1,0:T(8,128)S(1)} %bitcast.231, f32[64,128]{1,0:T(8,128)S(1)} %bitcast.243, f32[64,128]{1,0:T(8,128)S(1)} %bitcast.233, ...), kind=kOutput, calls=%fused_computation.35.clone.1 | convolution fusion | flops 51429376 | bytes 622596 | tf_op jit(solution)/shard_map/while/body/eval_jaxpr/gij,gcj->gci/dot_general | solution.py:36
  367.1 5.3 %fusion.117 = f32[64,128]{1,0:T(8,128)S(1)} fusion(f32[64,128]{1,0:T(8,128)S(1)} %bitcast.230, f32[64,128]{1,0:T(8,128)S(1)} %bitcast.242, f32[64,128]{1,0:T(8,128)S(1)} %bitcast.232, f32[64,128]{1,0:T(8,128)S(1)} %bitcast.244, f32[64,128]{1,0:T(8,128)S(1)} %bitcast.228, f32[64,128]{1,0:T(8,128)S(1)} %bitcast.240), kind=kLoop, calls=%fused_computation.32.clone.1 | loop fusion | flops 14671872 | bytes 229376 | tf_op jit(solution)/shard_map/while/body/eval_jaxpr/reduce_sum | solution.py:35
  372.4 10.3 %fusion.118 = f32[8,64,3,128]{3,2,1,0:T(4,128)S(1)} fusion(f32[8,64,3,128]{3,2,1,0:T(4,128)S(1)} %get-tuple-element.436, s32[]{:T(128)} %get-tuple-element.435, f32[64,3,128]{2,1,0:T(4,128)S(1)} %gather_fusion.2, f32[64,128]{1,0:T(8,128)S(1)} %bitcast.231, f32[64,128]{1,0:T(8,128)S(1)} %bitcast.243, f32[64,128]{1,0:T(8,128)S(1)} %bitcast.233, ...), kind=kOutput, calls=%fused_computation.35.clone.1 | convolution fusion | flops 51429376 | bytes 622596 | tf_op jit(solution)/shard_map/while/body/eval_jaxpr/gij,gcj->gci/dot_general | solution.py:36
  384.3 5.3 %fusion.117 = f32[64,128]{1,0:T(8,128)S(1)} fusion(f32[64,128]{1,0:T(8,128)S(1)} %bitcast.230, f32[64,128]{1,0:T(8,128)S(1)} %bitcast.242, f32[64,128]{1,0:T(8,128)S(1)} %bitcast.232, f32[64,128]{1,0:T(8,128)S(1)} %bitcast.244, f32[64,128]{1,0:T(8,128)S(1)} %bitcast.228, f32[64,128]{1,0:T(8,128)S(1)} %bitcast.240), kind=kLoop, calls=%fused_computation.32.clone.1 | loop fusion | flops 14671872 | bytes 229376 | tf_op jit(solution)/shard_map/while/body/eval_jaxpr/reduce_sum | solution.py:35
  389.6 10.3 %fusion.118 = f32[8,64,3,128]{3,2,1,0:T(4,128)S(1)} fusion(f32[8,64,3,128]{3,2,1,0:T(4,128)S(1)} %get-tuple-element.436, s32[]{:T(128)} %get-tuple-element.435, f32[64,3,128]{2,1,0:T(4,128)S(1)} %gather_fusion.2, f32[64,128]{1,0:T(8,128)S(1)} %bitcast.231, f32[64,128]{1,0:T(8,128)S(1)} %bitcast.243, f32[64,128]{1,0:T(8,128)S(1)} %bitcast.233, ...), kind=kOutput, calls=%fused_computation.35.clone.1 | convolution fusion | flops 51429376 | bytes 622596 | tf_op jit(solution)/shard_map/while/body/eval_jaxpr/gij,gcj->gci/dot_general | solution.py:36
  401.5 5.3 %fusion.117 = f32[64,128]{1,0:T(8,128)S(1)} fusion(f32[64,128]{1,0:T(8,128)S(1)} %bitcast.230, f32[64,128]{1,0:T(8,128)S(1)} %bitcast.242, f32[64,128]{1,0:T(8,128)S(1)} %bitcast.232, f32[64,128]{1,0:T(8,128)S(1)} %bitcast.244, f32[64,128]{1,0:T(8,128)S(1)} %bitcast.228, f32[64,128]{1,0:T(8,128)S(1)} %bitcast.240), kind=kLoop, calls=%fused_computation.32.clone.1 | loop fusion | flops 14671872 | bytes 229376 | tf_op jit(solution)/shard_map/while/body/eval_jaxpr/reduce_sum | solution.py:35
  406.8 10.3 %fusion.118 = f32[8,64,3,128]{3,2,1,0:T(4,128)S(1)} fusion(f32[8,64,3,128]{3,2,1,0:T(4,128)S(1)} %get-tuple-element.436, s32[]{:T(128)} %get-tuple-element.435, f32[64,3,128]{2,1,0:T(4,128)S(1)} %gather_fusion.2, f32[64,128]{1,0:T(8,128)S(1)} %bitcast.231, f32[64,128]{1,0:T(8,128)S(1)} %bitcast.243, f32[64,128]{1,0:T(8,128)S(1)} %bitcast.233, ...), kind=kOutput, calls=%fused_computation.35.clone.1 | convolution fusion | flops 51429376 | bytes 622596 | tf_op jit(solution)/shard_map/while/body/eval_jaxpr/gij,gcj->gci/dot_general | solution.py:36
  418.7 5.3 %fusion.117 = f32[64,128]{1,0:T(8,128)S(1)} fusion(f32[64,128]{1,0:T(8,128)S(1)} %bitcast.230, f32[64,128]{1,0:T(8,128)S(1)} %bitcast.242, f32[64,128]{1,0:T(8,128)S(1)} %bitcast.232, f32[64,128]{1,0:T(8,128)S(1)} %bitcast.244, f32[64,128]{1,0:T(8,128)S(1)} %bitcast.228, f32[64,128]{1,0:T(8,128)S(1)} %bitcast.240), kind=kLoop, calls=%fused_computation.32.clone.1 | loop fusion | flops 14671872 | bytes 229376 | tf_op jit(solution)/shard_map/while/body/eval_jaxpr/reduce_sum | solution.py:35
  424.0 10.3 %fusion.118 = f32[8,64,3,128]{3,2,1,0:T(4,128)S(1)} fusion(f32[8,64,3,128]{3,2,1,0:T(4,128)S(1)} %get-tuple-element.436, s32[]{:T(128)} %get-tuple-element.435, f32[64,3,128]{2,1,0:T(4,128)S(1)} %gather_fusion.2, f32[64,128]{1,0:T(8,128)S(1)} %bitcast.231, f32[64,128]{1,0:T(8,128)S(1)} %bitcast.243, f32[64,128]{1,0:T(8,128)S(1)} %bitcast.233, ...), kind=kOutput, calls=%fused_computation.35.clone.1 | convolution fusion | flops 51429376 | bytes 622596 | tf_op jit(solution)/shard_map/while/body/eval_jaxpr/gij,gcj->gci/dot_general | solution.py:36
  435.9 5.3 %fusion.117 = f32[64,128]{1,0:T(8,128)S(1)} fusion(f32[64,128]{1,0:T(8,128)S(1)} %bitcast.230, f32[64,128]{1,0:T(8,128)S(1)} %bitcast.242, f32[64,128]{1,0:T(8,128)S(1)} %bitcast.232, f32[64,128]{1,0:T(8,128)S(1)} %bitcast.244, f32[64,128]{1,0:T(8,128)S(1)} %bitcast.228, f32[64,128]{1,0:T(8,128)S(1)} %bitcast.240), kind=kLoop, calls=%fused_computation.32.clone.1 | loop fusion | flops 14671872 | bytes 229376 | tf_op jit(solution)/shard_map/while/body/eval_jaxpr/reduce_sum | solution.py:35
  441.2 10.3 %fusion.118 = f32[8,64,3,128]{3,2,1,0:T(4,128)S(1)} fusion(f32[8,64,3,128]{3,2,1,0:T(4,128)S(1)} %get-tuple-element.436, s32[]{:T(128)} %get-tuple-element.435, f32[64,3,128]{2,1,0:T(4,128)S(1)} %gather_fusion.2, f32[64,128]{1,0:T(8,128)S(1)} %bitcast.231, f32[64,128]{1,0:T(8,128)S(1)} %bitcast.243, f32[64,128]{1,0:T(8,128)S(1)} %bitcast.233, ...), kind=kOutput, calls=%fused_computation.35.clone.1 | convolution fusion | flops 51429376 | bytes 622596 | tf_op jit(solution)/shard_map/while/body/eval_jaxpr/gij,gcj->gci/dot_general | solution.py:36
  451.9 2.6 multiply_add_fusion
  (265 shorter events, 102.8 us)
Async XLA Ops:
  1.5 67.4 %collective-permute-start.1 = (f32[3,1,16,256]{3,2,1,0:T(8,128)S(1)}, f32[3,1,16,256]{3,2,1,0:T(8,128)S(1)}, u32[]{:S(2)}, u32[]{:S(2)}) collective-permute-start(f32[3,1,16,256]{3,2,1,0:T(8,128)S(1)} %get-tuple-element.220), channel_id=1, source_target_pairs={{0,4},{4,8},{8,12},{12,16},{16,20},{20,24},{24,28},{1,5},{5,9},{9,... | collective-permute-start | bytes 147464 | tf_op jit(solution)/shard_map/ppermute | solution.py:20
  6.4 62.5 %collective-permute-start = (f32[3,1,16,256]{3,2,1,0:T(8,128)S(1)}, f32[3,1,16,256]{3,2,1,0:T(8,128)S(1)}, u32[]{:S(2)}, u32[]{:S(2)}) collective-permute-start(f32[3,1,16,256]{3,2,1,0:T(8,128)S(1)} %get-tuple-element.219), channel_id=1, source_target_pairs={{4,0},{8,4},{12,8},{16,12},{20,16},{24,20},{28,24},{5,1},{9,5},{13... | collective-permute-start | bytes 147464 | tf_op jit(solution)/shard_map/ppermute | solution.py:22
  11.0 28.8 %all-to-all-start = ((s32[32,16,1]{1,2,0:T(1,128)}), s32[32,16,1]{1,2,0:T(1,128)S(1)}, u32[]{:S(2)}, u32[]{:S(2)}) async-start(s32[32,16,1]{1,2,0:T(1,128)} %bitcast.25), calls=%async_computation | async-start | bytes 32768 | tf_op jit(solution)/shard_map/all_to_all | solution.py:107
  19.3 18.8 %copy-start.20 = (s32[32]{0:T(128)S(1)}, s32[32]{0:T(128)}, u32[]{:S(2)}) copy-start(s32[32]{0:T(128)} %param.26) | copy-start | bytes 388
  37.1 8.5 %copy-start.18 = (s32[256,1]{0,1:T(1,128)S(1)}, s32[256,1]{0,1:T(1,128)}, u32[]{:S(2)}) copy-start(s32[256,1]{0,1:T(1,128)} %param.21) | copy-start | bytes 3076
  37.1 8.5 %copy-start.16 = (s32[2,512]{1,0:T(2,128)S(1)}, s32[2,512]{1,0:T(2,128)}, u32[]{:S(2)}) copy-start(s32[2,512]{1,0:T(2,128)} %param.25) | copy-start | bytes 12292
  37.2 8.5 %copy-start.17 = (s32[2,512]{1,0:T(2,128)S(1)}, s32[2,512]{1,0:T(2,128)}, u32[]{:S(2)}) copy-start(s32[2,512]{1,0:T(2,128)} %param.24) | copy-start | bytes 12292
  37.2 9.8 %copy-start.1 = (f32[256,3,128]{2,0,1:T(8,128)S(1)}, f32[256,3,128]{2,0,1:T(8,128)}, u32[]{:S(2)}) copy-start(f32[256,3,128]{2,0,1:T(8,128)} %param.19) | copy-start | bytes 1179652
  37.2 31.6 %copy-start.4 = (f32[3,8,16,256]{3,2,1,0:T(8,128)S(1)}, f32[3,8,16,256]{3,2,1,0:T(8,128)}, u32[]{:S(2)}) copy-start(f32[3,8,16,256]{3,2,1,0:T(8,128)} %param.18) | copy-start | bytes 1179652
  39.8 36.2 %all-to-all-start.1 = ((f32[512,4,128]{2,1,0:T(4,128)}), f32[512,4,128]{2,1,0:T(4,128)S(1)}, u32[]{:S(2)}, u32[]{:S(2)}) async-start(f32[512,4,128]{2,1,0:T(4,128)} %copy.60), calls=%async_computation.1 | async-start | bytes 2097152 | tf_op jit(solution)/shard_map/all_to_all | solution.py:108
  47.0 6.3 %copy-start.15 = (s32[1024]{0:T(1024)}, s32[1024]{0:T(1024)S(1)}, u32[]{:S(2)}) copy-start(s32[1024]{0:T(1024)S(1)} %get-tuple-element.236) | copy-start | bytes 12292
  47.6 21.1 %collective-permute-start.4 = (f32[16,3,128]{2,0,1:T(8,128)S(1)}, f32[16,3,128]{2,0,1:T(8,128)S(1)}, u32[]{:S(2)}, u32[]{:S(2)}) collective-permute-start(f32[16,3,128]{2,0,1:T(8,128)S(1)} %get-tuple-element.223), channel_id=1, source_target_pairs={{0,4},{4,8},{8,12},{12,16},{16,20},{20,24},{24,28},{28,0},{1,5},{5... | collective-permute-start | bytes 73736 | tf_op jit(solution)/shard_map/ppermute | solution.py:20
  49.5 19.3 %collective-permute-start.5 = (f32[16,3,128]{2,0,1:T(8,128)S(1)}, f32[16,3,128]{2,0,1:T(8,128)S(1)}, u32[]{:S(2)}, u32[]{:S(2)}) collective-permute-start(f32[16,3,128]{2,0,1:T(8,128)S(1)} %get-tuple-element.224), channel_id=1, source_target_pairs={{4,0},{8,4},{12,8},{16,12},{20,16},{24,20},{28,24},{0,28},{5,1},{9... | collective-permute-start | bytes 73736 | tf_op jit(solution)/shard_map/ppermute | solution.py:22
  68.8 7.2 %copy-start.8 = (f32[3,1,16,256]{3,2,1,0:T(8,128)}, f32[3,1,16,256]{3,2,1,0:T(8,128)S(1)}, u32[]{:S(2)}) copy-start(f32[3,1,16,256]{3,2,1,0:T(8,128)S(1)} %collective-permute-done.1) | copy-start | bytes 147460
  68.9 7.1 %copy-start.9 = (f32[3,1,16,256]{3,2,1,0:T(8,128)}, f32[3,1,16,256]{3,2,1,0:T(8,128)S(1)}, u32[]{:S(2)}) copy-start(f32[3,1,16,256]{3,2,1,0:T(8,128)S(1)} %collective-permute-done) | copy-start | bytes 147460
  68.9 11.0 %copy-start.3 = (f32[3,10,16,256]{3,2,1,0:T(8,128)}, f32[3,10,16,256]{3,2,1,0:T(8,128)S(1)}, u32[]{:S(2)}) copy-start(f32[3,10,16,256]{3,2,1,0:T(8,128)S(1)} %constant_dynamic-update-slice_fusion) | copy-start | bytes 1474564
  69.0 5.3 %collective-permute-start.2 = (f32[3,10,1,256]{3,2,1,0:T(1,128)S(1)}, f32[3,10,1,256]{3,2,1,0:T(1,128)S(1)}, u32[]{:S(2)}, u32[]{:S(2)}) collective-permute-start(f32[3,10,1,256]{3,2,1,0:T(1,128)S(1)} %get-tuple-element.218), channel_id=1, source_target_pairs={{1,0},{2,1},{3,2},{5,4},{6,5},{7,6},{9,8},{10,9},{11,10},{13,12},{... | collective-permute-start | bytes 92168 | tf_op jit(solution)/shard_map/ppermute | solution.py:22
  70.3 4.0 collective-permute-start.3
  74.3 1.7 copy-start.10
  74.3 1.7 copy-start.11
  79.9 2.3 copy-start
  82.2 5.2 %slice-start = ((f32[4,4,2,4,4,16,16]{6,5,4,2,0,3,1:T(8,128)}), f32[3,4,2,4,4,16,16]{6,5,4,2,0,3,1:T(8,128)S(1)}, s32[]{:S(2)}) async-start(f32[4,4,2,4,4,16,16]{6,5,4,2,0,3,1:T(8,128)} %copy-done), calls=%async_computation.3 | async-start | bytes 6291456 | tf_op jit(solution)/shard_map/slice | solution.py:118
  97.3 1.4 copy-start.2
  109.4 163.7 %all-to-all-start.2 = ((f32[512,4,128]{2,1,0:T(4,128)}), f32[512,4,128]{2,1,0:T(4,128)}, u32[]{:S(2)}, u32[]{:S(2)}) async-start(f32[512,4,128]{2,1,0:T(4,128)} %gather_fusion.5), calls=%async_computation.2 | async-start | bytes 2097152 | tf_op jit(solution)/shard_map/all_to_all | solution.py:131
  272.8 30.6 %copy-start.14 = (s32[1,512]{1,0:T(1,128)S(1)}, s32[1,512]{1,0:T(1,128)}, u32[]{:S(2)}) copy-start(s32[1,512]{1,0:T(1,128)} %get-tuple-element.231) | copy-start | bytes 6148
  272.8 30.6 %copy-start.19 = (f32[3]{0:T(128)S(1)}, f32[3]{0:T(128)}, u32[]{:S(2)}) copy-start(f32[3]{0:T(128)} %constant.101.clone) | copy-start | bytes 40
  272.9 30.5 %copy-start.5 = (f32[256,3,128]{2,0,1:T(8,128)S(1)}, f32[256,3,128]{2,0,1:T(8,128)}, u32[]{:S(2)}) copy-start(f32[256,3,128]{2,0,1:T(8,128)} %param.20) | copy-start | bytes 1179652
  275.6 36.1 %copy-start.12 = (s32[512]{0:T(512)S(1)}, s32[512]{0:T(512)}, u32[]{:S(2)}) copy-start(s32[512]{0:T(512)} %get-tuple-element.234) | copy-start | bytes 6148
  303.4 10.6 %copy-start.7 = (f32[256,128]{1,0:T(8,128)}, f32[256,128]{1,0:T(8,128)S(1)}, u32[]{:S(2)}) copy-start(f32[256,128]{1,0:T(8,128)S(1)} %fusion.74) | copy-start | bytes 393220
  306.9 6.6 %collective-permute-start.6 = (f32[16,3,128]{2,0,1:T(8,128)S(1)}, f32[16,3,128]{2,0,1:T(8,128)S(1)}, u32[]{:S(2)}, u32[]{:S(2)}) collective-permute-start(f32[16,3,128]{2,0,1:T(8,128)S(1)} %copy.81), channel_id=1, source_target_pairs={{0,4},{4,8},{8,12},{12,16},{16,20},{20,24},{24,28},{28,0},{1,5},{5... | collective-permute-start | bytes 73736 | tf_op jit(solution)/shard_map/ppermute | solution.py:20
  308.5 5.0 %collective-permute-start.7 = (f32[16,3,128]{2,0,1:T(8,128)S(1)}, f32[16,3,128]{2,0,1:T(8,128)S(1)}, u32[]{:S(2)}, u32[]{:S(2)}) collective-permute-start(f32[16,3,128]{2,0,1:T(8,128)S(1)} %copy.82), channel_id=1, source_target_pairs={{4,0},{8,4},{12,8},{16,12},{20,16},{24,20},{28,24},{0,28},{5,1},{9... | collective-permute-start | bytes 73736 | tf_op jit(solution)/shard_map/ppermute | solution.py:22
  314.0 137.9 %copy-start.6 = (f32[256,3,128]{2,0,1:T(8,128)S(1)}, f32[256,3,128]{2,0,1:T(8,128)}, u32[]{:S(2)}) copy-start(f32[256,3,128]{2,0,1:T(8,128)} %get-tuple-element.228) | copy-start | bytes 1179652
  314.0 137.9 %copy-start.13 = (s32[1,512]{1,0:T(1,128)S(1)}, s32[1,512]{1,0:T(1,128)}, u32[]{:S(2)}) copy-start(s32[1,512]{1,0:T(1,128)} %get-tuple-element.232) | copy-start | bytes 6148
where the time goes:
time: 457 us; the launch traced here: 454 us
  matrix products  204 us (45%)
  other arithmetic  101 us (22%)
  local copies, waits for them, and re-layouts  90 us (20%)
  starting transfers between devices  41.5 us (9%)
  waiting for transfers between devices  15.7 us (3%)
    dot_general x16, matrix products, pair_force(): jnp.einsum('gij,gcj->gci', coef, xb, precision=lax.Precision.HIGHEST)  165 us
    reduce_sum x16, other arithmetic, pair_force(): total = jnp.sum(coef, axis=2)  84.8 us
    gather x32, local copies, waits for them, and re-layouts, one_group(): return pair_force(extended[pair[0]], extended[pair[1]])  38 us
    dot_general x8, matrix products, pick_cells(): jnp.einsum('qkc,qic->qki', fluid_part, onehot, precision=lax.Precision.HI...  15.8 us
    ppermute x4, waiting for transfers between devices, padded_2(): lax.ppermute(tail, axis, [(i, (i + 1) % count) for i in range(ends)])  15.7 us
    dot_general x8, matrix products, histogram(): jnp.einsum('qki,qic->qkc', load_part, onehot, precision=lax.Precision.HIG...  11.7 us
    ppermute x4, starting transfers between devices, padded_2(): lax.ppermute(tail, axis, [(i, (i + 1) % count) for i in range(ends)])  11.3 us
  transfers between devices with their start and end apart: 11, of which 2 were waited for; matrix products, arithmetic and copies ran while one was open for 41% of the time, Pallas kernels for 0%

commit v1 on v0

--- a/solution.py
+++ b/solution.py
@@ -1,6 +1,11 @@
+import functools
+import math
+
 import jax
 import jax.numpy as jnp
 from jax import lax
+from jax.experimental import pallas as pl
+from jax.experimental.pallas import tpu as pltpu
 from jax.sharding import PartitionSpec as P
 
 SUBSTEPS = 2
@@ -25,16 +30,168 @@
         )
     return cells
 
-
-def pair_force(xa, xb):
-    dist2 = 0.0025 + (xa[:, 0, :, None] - xb[:, 0, None, :]) ** 2
-    dist2 = dist2 + (xa[:, 1, :, None] - xb[:, 1, None, :]) ** 2
-    dist2 = dist2 + (xa[:, 2, :, None] - xb[:, 2, None, :]) ** 2
-    dist = jnp.sqrt(dist2)
-    coef = 10.0 * jnp.maximum(0.25 - dist, 0.0) / dist
-    total = jnp.sum(coef, axis=2)
-    pulled = jnp.einsum("gij,gcj->gci", coef, xb, precision=lax.Precision.HIGHEST)
-    return xa * total[:, None, :] - pulled
+def split3(x):
+    one = x.astype(jnp.bfloat16).astype(jnp.float32)
+    rest = x - one
+    two = rest.astype(jnp.bfloat16).astype(jnp.float32)
+    return one, two, rest - two
+
+
+def push_kernel(unroll, selfs, others, pos, rims, push, near, far, loads, acc):
+    blocks = pos.shape[0]
+    pairs = selfs.shape[0]
+    size = pos.shape[2]
+    eye = (
+        lax.broadcasted_iota(jnp.int32, (size, size), 0)
+        == lax.broadcasted_iota(jnp.int32, (size, size), 1)
+    ).astype(jnp.float32).astype(jnp.bfloat16)
+    ones = jnp.ones((1, size), jnp.float32)
+    zeros = jnp.zeros((8, size), jnp.float32)
+
+    def side_other(q, raw):
+        x = (raw - 0.5) * 0.4
+        x1, x2, x3 = split3(x)
+        n1, n2, n3 = split3(jnp.sum(x * x, axis=0, keepdims=True))
+        rows = jnp.concatenate(
+            [x1, n1, x1, n2, x2, n3, x2, ones, x1, ones, x3, ones, zeros], axis=0
+        ).astype(jnp.bfloat16)
+        turned = lax.dot_general(
+            eye, rows, (((1,), (1,)), ((), ())), preferred_element_type=jnp.float32
+        )
+        far[q] = turned.astype(jnp.bfloat16)
+        loads[q] = jnp.concatenate([x1, ones, x2, ones * 0, x3, zeros[:5]], axis=0).astype(
+            jnp.bfloat16
+        )
+        return x1, x2, x3, n1, n2, n3
+
+    def own(q, carry):
+        raw = pos[q]
+        x1, x2, x3, _, _, _ = side_other(q, raw)
+        x = (raw - 0.5) * 0.4
+        n1, n2, n3 = split3(jnp.sum(x * x, axis=0, keepdims=True) + 0.0004)
+        y1, y2, y3 = -2.0 * x1, -2.0 * x2, -2.0 * x3
+        near[q] = jnp.concatenate(
+            [y1, ones, y2, ones, y1, ones, y2, n1, y3, n2, y1, n3, zeros], axis=0
+        ).astype(jnp.bfloat16)
+        acc[q] = jnp.zeros(acc.shape[1:], jnp.float32)
+        return carry
+
+    def rim(q, carry):
+        side_other(blocks + q, rims[q])
+        return carry
+
+    lax.fori_loop(0, blocks, own, 0, unroll=4)
+    lax.fori_loop(0, rims.shape[0], rim, 0, unroll=4)
+
+    def some(g, carry):
+        sums = []
+        for u in range(unroll):
+            a = selfs[g * unroll + u]
+            b = others[g * unroll + u]
+            dist2 = jnp.dot(far[b], near[a], preferred_element_type=jnp.float32)
+            w = jnp.maximum(lax.rsqrt(dist2) - 10.0, 0.0)
+            high = w.astype(jnp.bfloat16)
+            low = (w - high.astype(jnp.float32)).astype(jnp.bfloat16)
+            x = loads[b]
+            sums.append(
+                (
+                    a,
+                    jnp.dot(
+                        jnp.concatenate([x, x], axis=1),
+                        jnp.concatenate([high, low], axis=0),
+                        preferred_element_type=jnp.float32,
+                    ),
+                )
+            )
+        for a, total in sums:
+            acc[a] = acc[a] + total
+        return carry
+
+    lax.fori_loop(0, pairs // unroll, some, 0)
+
+    def finish(q, carry):
+        total = acc[q]
+        x = (pos[q] - 0.5) * 0.4
+        push[q] = 2.5 * (x * total[3:4] - (total[0:3] + total[4:7] + total[8:11]))
+        return carry
+
+    lax.fori_loop(0, blocks, finish, 0, unroll=4)
+
+
+def contact_push(selfs, others, position, rims):
+    blocks, comps, size = position.shape
+    ext = blocks + rims.shape[0]
+    pairs = selfs.shape[0]
+    unroll = math.gcd(pairs, 4)
+    vmem = pl.BlockSpec(memory_space=pltpu.VMEM)
+    smem = pl.BlockSpec(memory_space=pltpu.SMEM)
+    return pl.pallas_call(
+        functools.partial(push_kernel, unroll),
+        out_shape=jax.ShapeDtypeStruct(position.shape, jnp.float32),
+        in_specs=[smem, smem, vmem, vmem],
+        out_specs=vmem,
+        scratch_shapes=[
+            pltpu.VMEM((blocks, 32, size), jnp.bfloat16),
+            pltpu.VMEM((ext, size, 32), jnp.bfloat16),
+            pltpu.VMEM((ext, 16, size), jnp.bfloat16),
+            pltpu.VMEM((blocks, 16, size), jnp.float32),
+        ],
+        name="contact_push",
+    )(selfs, others, position, rims)
+
+
+def onehot_of(row):
+    size = row.shape[1]
+    return (lax.broadcasted_iota(jnp.int32, (size, size), 0) == row).astype(
+        jnp.float32
+    ).astype(jnp.bfloat16)
+
+
+def deposit_kernel(cells, vel, out):
+    size = cells.shape[1]
+    ones = jnp.ones((1, size), jnp.float32)
+    zeros = jnp.zeros((8, size), jnp.float32)
+
+    def block(q, carry):
+        v1, v2, v3 = split3(vel[q])
+        rows = jnp.concatenate([ones, v1, zeros[:1], v2, zeros[:1], v3, zeros[:4]], axis=0)
+        spots = onehot_of(cells[pl.ds(q, 1), :])
+        got = lax.dot_general(
+            rows.astype(jnp.bfloat16),
+            spots,
+            (((1,), (1,)), ((), ())),
+            preferred_element_type=jnp.float32,
+        )
+        out[q] = got[0:4] + got[4:8] + got[8:12]
+        return carry
+
+    lax.fori_loop(0, cells.shape[0], block, 0, unroll=4)
+
+
+def pick_kernel(cells, bricks, out):
+    zeros = jnp.zeros((4, cells.shape[1]), jnp.float32)
+
+    def block(q, carry):
+        v1, v2, v3 = split3(bricks[q])
+        rows = jnp.concatenate([v1, v2, v3, zeros], axis=0)
+        spots = onehot_of(cells[pl.ds(q, 1), :])
+        got = jnp.dot(rows.astype(jnp.bfloat16), spots, preferred_element_type=jnp.float32)
+        out[q] = got[0:4] + got[4:8] + got[8:12]
+        return carry
+
+    lax.fori_loop(0, cells.shape[0], block, 0, unroll=4)
+
+
+def per_block_call(kernel, name, cells, values):
+    vmem = pl.BlockSpec(memory_space=pltpu.VMEM)
+    blocks, size = cells.shape
+    return pl.pallas_call(
+        kernel,
+        out_shape=jax.ShapeDtypeStruct((blocks, 4, size), jnp.float32),
+        in_specs=[vmem, vmem],
+        out_specs=vmem,
+        name=name,
+    )(cells, values)
 
 
 def grid_bricks(grid):
@@ -77,18 +234,7 @@
     sizey = fluid_vel.shape[2]
     sizez = fluid_vel.shape[3]
     bricks = sizex // BRICK_X * (sizey // BRICK_Y) * (sizez // BRICK_Z)
-    loads = jnp.concatenate([jnp.ones((blocks, 1, per_brick), jnp.float32), part_vel], axis=1)
-    bunch = min(32, blocks)
-    cells_iota = jnp.arange(per_brick, dtype=jnp.int32)
-    cell_groups = cell_in_brick.reshape(blocks // bunch, bunch, per_brick)
-
-    def histogram(item):
-        load_part, cell_part = item
-        onehot = (cell_part[:, :, None] == cells_iota[None, None, :]).astype(jnp.float32)
-        return jnp.einsum("qki,qic->qkc", load_part, onehot, precision=lax.Precision.HIGHEST)
-
-    deposit = lax.map(histogram, (loads.reshape(blocks // bunch, bunch, 4, per_brick), cell_groups))
-    deposit = deposit.reshape(blocks, 4, per_brick)
+    deposit = per_block_call(deposit_kernel, "deposit", cell_in_brick, part_vel)
     target = brick_owner[:, 0]
     chosen = (target[:, None] == jnp.arange(tiles, dtype=jnp.int32)[None, :]).astype(jnp.float32)
     block_iota = jnp.arange(blocks, dtype=jnp.int32)
@@ -131,39 +277,18 @@
     back = lax.all_to_all(answer, ("gx", "gy"), split_axis=0, concat_axis=0, tiled=True)
     mine = back[slot]
 
-    def pick_cells(item):
-        fluid_part, cell_part = item
-        onehot = (cell_part[:, :, None] == cells_iota[None, None, :]).astype(jnp.float32)
-        return jnp.einsum("qkc,qic->qki", fluid_part, onehot, precision=lax.Precision.HIGHEST)
-
-    local_fluid = lax.map(
-        pick_cells, (mine.reshape(blocks // bunch, bunch, 4, per_brick), cell_groups)
-    )
-    local_fluid = local_fluid.reshape(blocks, 4, per_brick)
+    local_fluid = per_block_call(pick_kernel, "pick", cell_in_brick, mine)
     flow = local_fluid[:, :3, :]
     drift = 2.0 * local_fluid[:, 3:4, :]
     down = jnp.array([0.0, 0.0, -1.0], jnp.float32)[None, :, None]
     width = halo_list.shape[0] // 2
-    pair_count = pair_self.shape[1]
-    group = min(64, pair_count)
     position = part_pos
     velocity = part_vel
     for step in range(SUBSTEPS):
         outgoing = position[halo_list]
         rims = padded_2(outgoing, (("gx", 0),), width, True)
-        extended = jnp.concatenate([position, rims[:width], rims[3 * width :]], axis=0)
-        firsts = pair_self[step]
-        seconds = pair_other[step]
-
-        def one_group(pair):
-            return pair_force(extended[pair[0]], extended[pair[1]])
-
-        forces = lax.map(one_group, (firsts.reshape(-1, group), seconds.reshape(-1, group)))
-        forces = forces.reshape(pair_count, 3 * per_brick)
-        members = (firsts[None, :] == block_iota[:, None]).astype(jnp.float32)
-        push = jnp.dot(members, forces, precision=lax.Precision.HIGHEST).reshape(
-            blocks, 3, per_brick
-        )
+        rims = jnp.concatenate([rims[:width], rims[3 * width :]], axis=0)
+        push = contact_push(pair_self[step], pair_other[step], position, rims)
         velocity = velocity + 0.1 * (push + drift * (flow - velocity) + down)
         position = position + 0.1 * velocity
     return (fluid_new, position, velocity)

time: 457 us -> 275 us (0.60)
  matrix products: 204 us -> 5.47 us
  Pallas kernels: 0 us -> 140 us
  other arithmetic: 101 us -> 17.2 us
  local copies, waits for them, and re-layouts: 90 us -> 33.5 us
  waiting for transfers between devices: 15.7 us -> 31.6 us
    dot_general x34 -> x0, matrix products: 198 us -> none  [the longest x16 165 us: pair_force(): jnp.einsum('gij,gcj->gci', coef, xb, precision=lax.Precision.HIGHEST)]
    pallas_call x0 -> x4, Pallas kernels: none -> 140 us  [the longest x2 114 us: contact_push(): pl.pallas_call(functools.partial(push_kernel, unroll), out_shape=jax.Shap...]
    reduce_sum x16 -> x0, other arithmetic: 84.8 us -> none  [pair_force(): total = jnp.sum(coef, axis=2)]
    gather x32 -> x0, local copies, waits for them, and re-layouts: 38 us -> none  [one_group(): return pair_force(extended[pair[0]], extended[pair[1]])]
    eq x16 -> x0, local copies, waits for them, and re-layouts: 11.5 us -> none  [the longest x8 5.79 us: histogram(): cell_part[:, :, None] == cells_iota[None, None, :]]
    all_to_all x1, waiting for transfers between devices: 0.01 us -> 8.61 us  [per_device(): lax.all_to_all(send_dep, ('gx', 'gy'), split_axis=0, concat_axis=0, tiled...]
    dynamic_update_slice x8 -> x0, local copies, waits for them, and re-layouts: 5.26 us -> none  [per_device(): lax.map(histogram, (loads.reshape(blocks // bunch, bunch, 4, per_brick),...]
  transfers between devices with their start and end apart: 11 -> 11, of which waited for: 2 -> 5; matrix products, arithmetic and copies ran while one was open for 41% -> 4% of each run, Pallas kernels for 0% -> 26%
where the time goes in v1:
time: 275 us; the launch traced here: 274 us
  Pallas kernels  140 us (51%)
  starting transfers between devices  44.4 us (16%)
  local copies, waits for them, and re-layouts  33.5 us (12%)
  waiting for transfers between devices  31.6 us (11%)
  other arithmetic  17.2 us (6%)
  matrix products  5.47 us (2%)
    pallas_call x2, Pallas kernels, contact_push(): pl.pallas_call(functools.partial(push_kernel, unroll), out_shape=jax.Shap...  114 us
    pallas_call x2, Pallas kernels, per_block_call(): pl.pallas_call(kernel, out_shape=jax.ShapeDtypeStruct((blocks, 4, size),...  26 us
    ppermute x4, waiting for transfers between devices, padded_2(): lax.ppermute(tail, axis, [(i, (i + 1) % count) for i in range(ends)])  19.6 us
    all_to_all x1, starting transfers between devices, per_device(): lax.all_to_all(answer, ('gx', 'gy'), split_axis=0, concat_axis=0, tiled=T...  12.4 us
    ppermute x4, starting transfers between devices, padded_2(): lax.ppermute(head, axis, [((i + 1) % count, i) for i in range(ends)])  10.3 us
    all_to_all x1, waiting for transfers between devices, per_device(): lax.all_to_all(send_dep, ('gx', 'gy'), split_axis=0, concat_axis=0, tiled...  8.61 us
    ppermute x4, starting transfers between devices, padded_2(): lax.ppermute(tail, axis, [(i, (i + 1) % count) for i in range(ends)])  8.59 us
    all_to_all x1, starting transfers between devices, per_device(): lax.all_to_all(send_ids, ('gx', 'gy'), split_axis=0, concat_axis=0, tiled...  7.33 us
  transfers between devices with their start and end apart: 11, of which 5 were waited for; matrix products, arithmetic and copies ran while one was open for 4% of the time, Pallas kernels for 26%

profile of v1, /device:TPU:0, one launch (start us, length us, event | category | flops | bytes accessed | tf_op | source)
XLA Modules:
  0.0 273.7 jit_solution(3893774106049600085)
XLA Ops:
  0.6 1.0 fusion
  1.6 0.7 multiply_add_fusion.5
  2.3 0.7 convert_element_type.30
  3.0 0.3 fusion.3
  3.3 0.7 all_to_all.14
  4.0 7.3 %all-to-all-start = ((s32[32,16,1]{1,2,0:T(1,128)}), s32[32,16,1]{1,2,0:T(1,128)S(1)}, u32[]{:S(2)}, u32[]{:S(2)}) async-start(s32[32,16,1]{1,2,0:T(1,128)} %bitcast.3), calls=%async_computation | async-start | bytes 32768 | tf_op jit(solution)/shard_map/all_to_all | solution.py:253
  11.3 2.0 copy.54.vel
  13.4 14.2 %deposit.1 = f32[256,4,128]{2,1,0:T(4,128)} custom-call(s32[256,128]{1,0:T(8,128)} %cells.3, f32[256,3,128]{2,1,0:T(4,128)} %copy.54.vel), custom_call_target="tpu_custom_call" | custom-call | tf_op jit(solution)/shard_map/deposit/pallas_call | solution.py:188
  27.6 1.1 copy.84
  28.7 0.2 copy.55
  28.9 0.7 fusion.4
  29.6 1.7 copy.56
  31.2 5.8 %all-to-all-start.1 = ((f32[512,4,128]{2,1,0:T(4,128)}), f32[512,4,128]{2,1,0:T(4,128)S(1)}, u32[]{:S(2)}, u32[]{:S(2)}) async-start(f32[512,4,128]{2,1,0:T(4,128)} %copy.56), calls=%async_computation.1 | async-start | bytes 2097152 | tf_op jit(solution)/shard_map/all_to_all | solution.py:254
  37.1 3.7 %collective-permute-start.1 = (f32[3,1,16,256]{3,2,1,0:T(8,128)S(1)}, f32[3,1,16,256]{3,2,1,0:T(8,128)S(1)}, u32[]{:S(2)}, u32[]{:S(2)}) collective-permute-start(f32[3,1,16,256]{3,2,1,0:T(8,128)S(1)} %get-tuple-element.22), channel_id=1, source_target_pairs={{0,4},{4,8},{8,12},{12,16},{16,20},{20,24},{24,28},{1,5},{5,9},{9,... | collective-permute-start | bytes 147464 | tf_op jit(solution)/shard_map/ppermute | solution.py:25
  40.8 1.3 collective-permute-start
  42.1 0.1 all_to_all.17
  42.2 2.2 collective-permute-done.1
  44.4 3.4 %collective-permute-done = f32[3,1,16,256]{3,2,1,0:T(8,128)S(1)} collective-permute-done((f32[3,1,16,256]{3,2,1,0:T(8,128)S(1)}, f32[3,1,16,256]{3,2,1,0:T(8,128)S(1)}, u32[]{:S(2)}, u32[]{:S(2)}) %collective-permute-start) | collective-permute-done | bytes 49184 | tf_op jit(solution)/shard_map/ppermute | solution.py:27
  47.9 1.3 collective-permute-start.2
  49.2 3.0 %collective-permute-start.3 = (f32[3,10,1,256]{3,2,1,0:T(1,128)S(1)}, f32[3,10,1,256]{3,2,1,0:T(1,128)S(1)}, u32[]{:S(2)}, u32[]{:S(2)}) collective-permute-start(f32[3,10,1,256]{3,2,1,0:T(1,128)S(1)} %get-tuple-element.19), channel_id=1, source_target_pairs={{0,1},{1,2},{2,3},{4,5},{5,6},{6,7},{8,9},{9,10},{10,11},{12,13},{... | collective-permute-start | bytes 92168 | tf_op jit(solution)/shard_map/ppermute | solution.py:25
  52.3 0.5 broadcast.149
  52.8 0.7 reduce.5
  53.5 0.1 eq.71
  53.6 1.6 select_maximum_fusion
  55.2 8.6 %all-to-all-done.1 = f32[512,4,128]{2,1,0:T(4,128)S(1)} async-done(((f32[512,4,128]{2,1,0:T(4,128)}), f32[512,4,128]{2,1,0:T(4,128)S(1)}, u32[]{:S(2)}, u32[]{:S(2)}) %all-to-all-start.1) | async-done | bytes 1048608 | tf_op jit(solution)/shard_map/all_to_all | solution.py:254
  63.8 0.4 copy.57
  64.2 3.5 %convolution_bitcast_fusion = f32[4,4,2,4,4,16,16]{6,5,4,2,0,3,1:T(8,128)S(1)} fusion(f32[4,2,4,16,512,1,1]{4,3,2,1,0,6,5:T(8,128)S(1)} %bitcast.59, s32[512]{0:T(512)S(1)} %eq.71, s32[4,4,16]{2,1,0:T(4,128)S(1)} %multiply_add_fusion.4), kind=kOutput, calls=%fused_computation.5 | convolution fusion | flops 805437440 | bytes 1575936 | tf_op jit(solution)/shard_map/dot_general | solution.py:259
  67.7 1.4 multiply_divide_fusion
  69.1 0.4 slice.116
  69.5 1.1 copy.58
  70.6 2.3 squeeze.19
  72.9 1.6 divide_multiply_fusion
  74.5 1.9 copy.59
  76.4 3.1 %slice.92 = f32[3,8,16,256]{3,2,1,0:T(8,128)S(1)} reshape(f32[3,4,2,4,4,16,16]{6,5,4,3,2,1,0:T(8,128)} %copy.59) | data formatting | bytes 786432 | tf_op jit(solution)/shard_map/slice | solution.py:264
  79.6 1.1 fusion.11
  80.8 1.9 concatenate.37
  82.7 1.4 copy.63
  84.1 0.4 copy.64
  84.5 3.1 %maximum_bitcast_fusion = f32[4,4,16,4,2,4,16]{6,5,4,2,1,0,3:T(4,128)} fusion(f32[1,4,2,4,4,16,16]{6,4,2,5,3,1,0:T(4,128)S(1)} %copy.64, f32[3,4,2,4,4,16,16]{6,4,2,5,3,1,0:T(4,128)S(1)} %copy.63), kind=kLoop, calls=%fused_computation.4 | loop fusion | flops 131072 | bytes 1048576 | tf_op jit(solution)/shard_map/transpose | solution.py:202
  87.6 4.2 %reshape.118 = f32[256,4,128]{2,0,1:T(8,128)S(1)} reshape(f32[4,4,16,4,2,4,16]{6,5,4,2,1,0,3:T(4,128)} %maximum_bitcast_fusion) | data formatting | bytes 1048576 | tf_op jit(solution)/shard_map/reshape | solution.py:203
  91.9 0.3 copy.65
  92.2 2.7 gather_fusion.1
  94.9 12.4 %all-to-all-start.2 = ((f32[512,4,128]{2,1,0:T(4,128)}), f32[512,4,128]{2,1,0:T(4,128)S(1)}, u32[]{:S(2)}, u32[]{:S(2)}) async-start(f32[512,4,128]{2,1,0:T(4,128)} %gather_fusion.1), calls=%async_computation.2 | async-start | bytes 2097152 | tf_op jit(solution)/shard_map/all_to_all | solution.py:277
  107.3 0.6 fusion.25
  107.9 0.6 fusion.24
  108.5 0.6 gather_fusion
  109.2 1.8 collective-permute-start.4
  111.0 3.0 %collective-permute-start.5 = (f32[16,3,128]{2,1,0:T(4,128)S(1)}, f32[16,3,128]{2,1,0:T(4,128)S(1)}, u32[]{:S(2)}, u32[]{:S(2)}) collective-permute-start(f32[16,3,128]{2,1,0:T(4,128)S(1)} %copy.74), channel_id=1, source_target_pairs={{4,0},{8,4},{12,8},{16,12},{20,16},{24,20},{28,24},{0,28},{5,1},{9... | collective-permute-start | bytes 73736 | tf_op jit(solution)/shard_map/ppermute | solution.py:27
  114.0 1.1 copy.68.pos
  115.1 15.5 %collective-permute-done.4 = f32[16,3,128]{2,1,0:T(4,128)S(1)} collective-permute-done((f32[16,3,128]{2,1,0:T(4,128)S(1)}, f32[16,3,128]{2,1,0:T(4,128)S(1)}, u32[]{:S(2)}, u32[]{:S(2)}) %collective-permute-start.4) | collective-permute-done | bytes 24608 | tf_op jit(solution)/shard_map/ppermute | solution.py:25
  130.6 0.6 pad_maximum_fusion.4.rims
  131.3 57.0 %contact_push.2 = f32[256,3,128]{2,1,0:T(4,128)} custom-call(s32[512]{0:T(512)} %bitcast.63, s32[512]{0:T(512)} %bitcast.64, f32[256,3,128]{2,1,0:T(4,128)} %copy.68.pos, f32[32,3,128]{2,1,0:T(4,128)} %pad_maximum_fusion.4.rims), custom_call_target="tpu_custom_call" | custom-call | tf_op jit(solution)/shard_map/contact_push/pallas_call | solution.py:128
  188.3 1.8 gather_fusion.2
  190.1 11.8 %pick.1 = f32[256,4,128]{2,1,0:T(4,128)} custom-call(s32[256,128]{1,0:T(8,128)} %cells.3, f32[256,4,128]{2,1,0:T(4,128)} %gather_fusion.2), custom_call_target="tpu_custom_call" | custom-call | tf_op jit(solution)/shard_map/pick/pallas_call | solution.py:188
  201.9 1.2 slice_multiply_fusion
  203.2 1.8 multiply_add_fusion.2.pos
  205.0 0.6 gather_fusion.3
  205.7 4.7 %collective-permute-start.7 = (f32[16,3,128]{2,1,0:T(4,128)S(1)}, f32[16,3,128]{2,1,0:T(4,128)S(1)}, u32[]{:S(2)}, u32[]{:S(2)}) collective-permute-start(f32[16,3,128]{2,1,0:T(4,128)S(1)} %get-tuple-element.24), channel_id=1, source_target_pairs={{4,0},{8,4},{12,8},{16,12},{20,16},{24,20},{28,24},{0,28},{5,1},{9... | collective-permute-start | bytes 73736 | tf_op jit(solution)/shard_map/ppermute | solution.py:27
  210.4 1.9 collective-permute-done.6
  212.3 0.6 pad_maximum_fusion.5.rims
  212.9 57.2 %contact_push.3 = f32[256,3,128]{2,1,0:T(4,128)} custom-call(s32[512]{0:T(512)} %bitcast.61, s32[512]{0:T(512)} %bitcast.62, f32[256,3,128]{2,1,0:T(4,128)} %copy-done.1, f32[32,3,128]{2,1,0:T(4,128)} %pad_maximum_fusion.5.rims), custom_call_target="tpu_custom_call" | custom-call | tf_op jit(solution)/shard_map/contact_push/pallas_call | solution.py:128
  270.2 1.9 multiply_add_fusion
  272.1 0.8 copy.69
  272.9 0.8 copy.70
  (74 shorter events, 0.4 us)
Async XLA Ops:
  4.0 27.2 %all-to-all-start = ((s32[32,16,1]{1,2,0:T(1,128)}), s32[32,16,1]{1,2,0:T(1,128)S(1)}, u32[]{:S(2)}, u32[]{:S(2)}) async-start(s32[32,16,1]{1,2,0:T(1,128)} %bitcast.3), calls=%async_computation | async-start | bytes 32768 | tf_op jit(solution)/shard_map/all_to_all | solution.py:253
  31.2 5.9 %copy-start.9 = (f32[3,8,16,256]{3,2,1,0:T(8,128)S(1)}, f32[3,8,16,256]{3,2,1,0:T(8,128)}, u32[]{:S(2)}) copy-start(f32[3,8,16,256]{3,2,1,0:T(8,128)} %param.10) | copy-start | bytes 1179652
  31.2 10.9 %copy-start.24 = (s32[32]{0:T(128)S(1)}, s32[32]{0:T(128)}, u32[]{:S(2)}) copy-start(s32[32]{0:T(128)} %param.18) | copy-start | bytes 388
  31.2 32.6 %all-to-all-start.1 = ((f32[512,4,128]{2,1,0:T(4,128)}), f32[512,4,128]{2,1,0:T(4,128)S(1)}, u32[]{:S(2)}, u32[]{:S(2)}) async-start(f32[512,4,128]{2,1,0:T(4,128)} %copy.56), calls=%async_computation.1 | async-start | bytes 2097152 | tf_op jit(solution)/shard_map/all_to_all | solution.py:254
  37.1 7.3 %collective-permute-start.1 = (f32[3,1,16,256]{3,2,1,0:T(8,128)S(1)}, f32[3,1,16,256]{3,2,1,0:T(8,128)S(1)}, u32[]{:S(2)}, u32[]{:S(2)}) collective-permute-start(f32[3,1,16,256]{3,2,1,0:T(8,128)S(1)} %get-tuple-element.22), channel_id=1, source_target_pairs={{0,4},{4,8},{8,12},{12,16},{16,20},{20,24},{24,28},{1,5},{5,9},{9,... | collective-permute-start | bytes 147464 | tf_op jit(solution)/shard_map/ppermute | solution.py:25
  40.8 7.0 %collective-permute-start = (f32[3,1,16,256]{3,2,1,0:T(8,128)S(1)}, f32[3,1,16,256]{3,2,1,0:T(8,128)S(1)}, u32[]{:S(2)}, u32[]{:S(2)}) collective-permute-start(f32[3,1,16,256]{3,2,1,0:T(8,128)S(1)} %get-tuple-element.21), channel_id=1, source_target_pairs={{4,0},{8,4},{12,8},{16,12},{20,16},{24,20},{28,24},{5,1},{9,5},{13... | collective-permute-start | bytes 147464 | tf_op jit(solution)/shard_map/ppermute | solution.py:27
  44.4 10.8 %copy-start.12 = (f32[3,1,16,256]{3,2,1,0:T(8,128)}, f32[3,1,16,256]{3,2,1,0:T(8,128)S(1)}, u32[]{:S(2)}) copy-start(f32[3,1,16,256]{3,2,1,0:T(8,128)S(1)} %collective-permute-done.1) | copy-start | bytes 147460
  47.8 7.4 %copy-start.14 = (f32[3,1,16,256]{3,2,1,0:T(8,128)}, f32[3,1,16,256]{3,2,1,0:T(8,128)S(1)}, u32[]{:S(2)}) copy-start(f32[3,1,16,256]{3,2,1,0:T(8,128)S(1)} %collective-permute-done) | copy-start | bytes 147460
  47.9 16.3 %copy-start.7 = (f32[3,10,16,256]{3,2,1,0:T(8,128)}, f32[3,10,16,256]{3,2,1,0:T(8,128)S(1)}, u32[]{:S(2)}) copy-start(f32[3,10,16,256]{3,2,1,0:T(8,128)S(1)} %constant_dynamic-update-slice_fusion) | copy-start | bytes 1474564
  47.9 5.6 %collective-permute-start.2 = (f32[3,10,1,256]{3,2,1,0:T(1,128)S(1)}, f32[3,10,1,256]{3,2,1,0:T(1,128)S(1)}, u32[]{:S(2)}, u32[]{:S(2)}) collective-permute-start(f32[3,10,1,256]{3,2,1,0:T(1,128)S(1)} %get-tuple-element.20), channel_id=1, source_target_pairs={{1,0},{2,1},{3,2},{5,4},{6,5},{7,6},{9,8},{10,9},{11,10},{13,12},{... | collective-permute-start | bytes 92168 | tf_op jit(solution)/shard_map/ppermute | solution.py:27
  49.2 4.4 %collective-permute-start.3 = (f32[3,10,1,256]{3,2,1,0:T(1,128)S(1)}, f32[3,10,1,256]{3,2,1,0:T(1,128)S(1)}, u32[]{:S(2)}, u32[]{:S(2)}) collective-permute-start(f32[3,10,1,256]{3,2,1,0:T(1,128)S(1)} %get-tuple-element.19), channel_id=1, source_target_pairs={{0,1},{1,2},{2,3},{4,5},{5,6},{6,7},{8,9},{9,10},{10,11},{12,13},{... | collective-permute-start | bytes 92168 | tf_op jit(solution)/shard_map/ppermute | solution.py:25
  53.6 1.6 copy-start.16
  53.6 1.6 copy-start.18
  76.4 3.2 %copy-start.6 = (f32[3,10,18,258]{3,2,1,0:T(8,128)S(1)}, f32[3,10,18,258]{3,2,1,0:T(8,128)}, u32[]{:S(2)}) copy-start(f32[3,10,18,258]{3,2,1,0:T(8,128)} %select_maximum_fusion) | copy-start | bytes 1671844
  76.4 3.2 %copy-start.8 = (f32[3,10,16,256]{3,2,1,0:T(8,128)S(1)}, f32[3,10,16,256]{3,2,1,0:T(8,128)}, u32[]{:S(2)}) copy-start(f32[3,10,16,256]{3,2,1,0:T(8,128)} %copy-done.7) | copy-start | bytes 1474564
  76.4 3.2 %copy-start.10 = (f32[8,16,256]{2,1,0:T(8,128)S(1)}, f32[8,16,256]{2,1,0:T(8,128)}, u32[]{:S(2)}) copy-start(f32[8,16,256]{2,1,0:T(8,128)} %squeeze.19) | copy-start | bytes 393220
  76.4 3.2 %copy-start.11 = (f32[8,16,256]{2,1,0:T(8,128)S(1)}, f32[8,16,256]{2,1,0:T(8,128)}, u32[]{:S(2)}) copy-start(f32[8,16,256]{2,1,0:T(8,128)} %divide_multiply_fusion) | copy-start | bytes 393220
  76.4 3.2 %copy-start.13 = (f32[3,1,16,256]{3,2,1,0:T(8,128)S(1)}, f32[3,1,16,256]{3,2,1,0:T(8,128)}, u32[]{:S(2)}) copy-start(f32[3,1,16,256]{3,2,1,0:T(8,128)} %copy-done.12) | copy-start | bytes 147460
  76.4 3.2 %copy-start.15 = (f32[3,1,16,256]{3,2,1,0:T(8,128)S(1)}, f32[3,1,16,256]{3,2,1,0:T(8,128)}, u32[]{:S(2)}) copy-start(f32[3,1,16,256]{3,2,1,0:T(8,128)} %copy-done.14) | copy-start | bytes 147460
  76.4 3.2 %copy-start.17 = (f32[3,10,1,256]{3,2,1,0:T(1,128)S(1)}, f32[3,10,1,256]{3,2,1,0:T(1,128)}, u32[]{:S(2)}) copy-start(f32[3,10,1,256]{3,2,1,0:T(1,128)} %copy-done.16) | copy-start | bytes 92164
  76.4 3.2 %copy-start.19 = (f32[3,10,1,256]{3,2,1,0:T(1,128)S(1)}, f32[3,10,1,256]{3,2,1,0:T(1,128)}, u32[]{:S(2)}) copy-start(f32[3,10,1,256]{3,2,1,0:T(1,128)} %copy-done.18) | copy-start | bytes 92164
  82.7 1.4 copy-start.4
  94.9 12.4 %copy-start.20 = (s32[256,1]{0,1:T(1,128)S(1)}, s32[256,1]{0,1:T(1,128)}, u32[]{:S(2)}) copy-start(s32[256,1]{0,1:T(1,128)} %param.13) | copy-start | bytes 3076
  94.9 12.4 %copy-start.21 = (s32[2,512]{1,0:T(2,128)S(1)}, s32[2,512]{1,0:T(2,128)}, u32[]{:S(2)}) copy-start(s32[2,512]{1,0:T(2,128)} %param.16) | copy-start | bytes 12292
  94.9 13.0 %copy-start.22 = (s32[2,512]{1,0:T(2,128)S(1)}, s32[2,512]{1,0:T(2,128)}, u32[]{:S(2)}) copy-start(s32[2,512]{1,0:T(2,128)} %param.17) | copy-start | bytes 12292
  94.9 13.6 %copy-start.3 = (f32[256,3,128]{2,0,1:T(8,128)S(1)}, f32[256,3,128]{2,0,1:T(8,128)}, u32[]{:S(2)}) copy-start(f32[256,3,128]{2,0,1:T(8,128)} %param.11) | copy-start | bytes 1179652
  94.9 93.4 %all-to-all-start.2 = ((f32[512,4,128]{2,1,0:T(4,128)}), f32[512,4,128]{2,1,0:T(4,128)S(1)}, u32[]{:S(2)}, u32[]{:S(2)}) async-start(f32[512,4,128]{2,1,0:T(4,128)} %gather_fusion.1), calls=%async_computation.2 | async-start | bytes 2097152 | tf_op jit(solution)/shard_map/all_to_all | solution.py:277
  109.2 21.4 %collective-permute-start.4 = (f32[16,3,128]{2,1,0:T(4,128)S(1)}, f32[16,3,128]{2,1,0:T(4,128)S(1)}, u32[]{:S(2)}, u32[]{:S(2)}) collective-permute-start(f32[16,3,128]{2,1,0:T(4,128)S(1)} %copy.73), channel_id=1, source_target_pairs={{0,4},{4,8},{8,12},{12,16},{16,20},{20,24},{24,28},{28,0},{1,5},{5... | collective-permute-start | bytes 73736 | tf_op jit(solution)/shard_map/ppermute | solution.py:25
  111.0 19.6 %collective-permute-start.5 = (f32[16,3,128]{2,1,0:T(4,128)S(1)}, f32[16,3,128]{2,1,0:T(4,128)S(1)}, u32[]{:S(2)}, u32[]{:S(2)}) collective-permute-start(f32[16,3,128]{2,1,0:T(4,128)S(1)} %copy.74), channel_id=1, source_target_pairs={{4,0},{8,4},{12,8},{16,12},{20,16},{24,20},{28,24},{0,28},{5,1},{9... | collective-permute-start | bytes 73736 | tf_op jit(solution)/shard_map/ppermute | solution.py:27
  188.3 14.8 %copy-start.2 = (f32[256,3,128]{2,1,0:T(4,128)S(1)}, f32[256,3,128]{2,1,0:T(4,128)}, u32[]{:S(2)}) copy-start(f32[256,3,128]{2,1,0:T(4,128)} %contact_push.2) | copy-start | bytes 1179652
  188.3 14.8 %copy-start.5 = (f32[256,3,128]{2,0,1:T(8,128)S(1)}, f32[256,3,128]{2,0,1:T(8,128)}, u32[]{:S(2)}) copy-start(f32[256,3,128]{2,0,1:T(8,128)} %param.12) | copy-start | bytes 1179652
  188.3 14.9 %copy-start.23 = (f32[3]{0:T(128)S(1)}, f32[3]{0:T(128)}, u32[]{:S(2)}) copy-start(f32[3]{0:T(128)} %constant.37.clone) | copy-start | bytes 40
  205.0 8.0 %copy-start.1 = (f32[256,3,128]{2,1,0:T(4,128)}, f32[256,3,128]{2,1,0:T(4,128)S(1)}, u32[]{:S(2)}) copy-start(f32[256,3,128]{2,1,0:T(4,128)S(1)} %multiply_add_fusion.2.pos) | copy-start | bytes 1179652
  205.0 65.2 %copy-start = (f32[256,4,128]{2,1,0:T(4,128)S(1)}, f32[256,4,128]{2,1,0:T(4,128)}, u32[]{:S(2)}) copy-start(f32[256,4,128]{2,1,0:T(4,128)} %pick.1) | copy-start | bytes 1572868
  205.6 6.7 %collective-permute-start.6 = (f32[16,3,128]{2,1,0:T(4,128)S(1)}, f32[16,3,128]{2,1,0:T(4,128)S(1)}, u32[]{:S(2)}, u32[]{:S(2)}) collective-permute-start(f32[16,3,128]{2,1,0:T(4,128)S(1)} %get-tuple-element.23), channel_id=1, source_target_pairs={{0,4},{4,8},{8,12},{12,16},{16,20},{20,24},{24,28},{28,0},{1,5},{5... | collective-permute-start | bytes 73736 | tf_op jit(solution)/shard_map/ppermute | solution.py:25
  205.7 6.6 %collective-permute-start.7 = (f32[16,3,128]{2,1,0:T(4,128)S(1)}, f32[16,3,128]{2,1,0:T(4,128)S(1)}, u32[]{:S(2)}, u32[]{:S(2)}) collective-permute-start(f32[16,3,128]{2,1,0:T(4,128)S(1)} %get-tuple-element.24), channel_id=1, source_target_pairs={{4,0},{8,4},{12,8},{16,12},{20,16},{24,20},{28,24},{0,28},{5,1},{9... | collective-permute-start | bytes 73736 | tf_op jit(solution)/shard_map/ppermute | solution.py:27
